TPU v7x, 32 devices: a whole 2x2x4 slice. The times are simulated.
32 devices in a mesh: dp: 8 (over y, x, core), tensor: 4 (over z).
Axes of the slice: x: 2, y: 2, z: 4, core: 2. Of those that a mesh axis runs over, the one named last changes fastest.
Arguments:
- tokens: bfloat16 [16384, 1536], P('dp'), may hold values from -6 to 6
- cotangent: bfloat16 [16384, 1536], P('dp'), may hold values from -6 to 6
- destination: int32 [16384], P('dp'), may hold values from 0 to 16383, as said below
- lengths: int32 [8, 4], P('dp'), may hold values from 1 to 1024, 2048 in all within a row
- norm_gain: float32 [1536], replicated, may hold values from 0.1 to 1.9
- inner_weight: float32 [1536, 2, 3072], P('dp', None, 'tensor'), may hold values from -0.15625 to 0.15625
- shared_weight: float32 [1536, 256], P('dp'), may hold values from -0.15625 to 0.15625
- step_weight: float32 [1536, 48], P('dp', 'tensor'), may hold values from -0.15625 to 0.15625
- filter_weight: float32 [4, 3072], P(None, 'tensor'), may hold values from -3 to 3
- filter_bias: float32 [3072], P('tensor'), may hold values from -3 to 3
- shared_filter: float32 [4, 256], replicated, may hold values from -3 to 3
- shared_filter_bias: float32 [256], replicated, may hold values from -3 to 3
- step_bias: float32 [48], P('tensor'), may hold values from -6 to -2
- decay_log: float32 [48], P('tensor'), may hold values from 0 to 2.77
- skip_gain: float32 [48], P('tensor'), may hold values from 0.5 to 1.5
- gate_gain: float32 [3072], P('tensor'), may hold values from 0.1 to 1.9
- out_weight: float32 [1536, 3072], P('dp', 'tensor'), may hold values from -0.109375 to 0.109375
Outputs:
- layer_out: bfloat16 [16384, 1536], P('dp')
- input_grad: bfloat16 [16384, 1536], P('dp')
- norm_gain_grad: float32 [1536], replicated
- inner_weight_grad: float32 [1536, 2, 3072], P('dp', None, 'tensor')
- shared_weight_grad: float32 [1536, 256], P('dp')
- step_weight_grad: float32 [1536, 48], P('dp', 'tensor')
- filter_weight_grad: float32 [4, 3072], P(None, 'tensor')
- filter_bias_grad: float32 [3072], P('tensor')
- shared_filter_grad: float32 [4, 256], replicated
- shared_filter_bias_grad: float32 [256], replicated
- step_bias_grad: float32 [48], P('tensor')
- decay_log_grad: float32 [48], P('tensor')
- skip_gain_grad: float32 [48], P('tensor')
- gate_gain_grad: float32 [3072], P('tensor')
- out_weight_grad: float32 [1536, 3072], P('dp', 'tensor')
Inputs may be any that keep to these rules, and one draw needn't show every extreme that they name: destination is a permutation. The tokens at given positions s * 2048 to (s + 1) * 2048 - 1 that go to work block w take exactly the work positions w * 2048 + s * 256 to w * 2048 + (s + 1) * 256 - 1. `lengths`: each row sums to 2048, and its longest sequence has exactly 1024 tokens.
All inputs are finite; a program needn't handle non-finite values.
Results may differ from a plain program's by a relative error of at most 0.012.
Values may be sent and summed in bfloat16 or wider, within the bound.
No kernel may reach another device: no remote copies, remote signals or barrier semaphores. Data moves between devices by JAX's collectives and lax.ppermute only.
A program may use at most 256 MiB of HBM per device.

v0:
```python
import jax
import jax.numpy as jnp
from jax import lax
from jax.sharding import PartitionSpec as P

INNER = 3072
SPAN = 256
EPSILON = 1e-05
PRECISE = lax.Precision.HIGHEST


def segments_of(lengths, row_count):
    seq_ends = jnp.cumsum(lengths)
    seq_starts = seq_ends - lengths
    places = jnp.arange(row_count, dtype=jnp.int32)
    segment = jnp.sum((places[:, None] >= seq_ends[None, :]).astype(jnp.int32), axis=1)
    belongs = segment[:, None] == jnp.arange(lengths.shape[0], dtype=jnp.int32)[None, :]
    position = places - jnp.sum(jnp.where(belongs, seq_starts[None, :], 0), axis=1)
    return (segment, position)


def causal_filter(signal, kernel, offset_bias, position):
    result = offset_bias + kernel[0] * signal
    for offset in range(1, kernel.shape[0]):
        shifted = jnp.pad(signal, ((offset, 0), (0, 0)))[: signal.shape[0]]
        allowed = (position >= offset).astype(signal.dtype)
        result = result + kernel[offset] * shifted * allowed[:, None]
    return result


def mixer(
    inputs,
    shared,
    step_raw,
    filter_weight,
    filter_bias,
    shared_filter,
    shared_filter_bias,
    step_bias,
    decay_log,
    skip_gain,
    segment,
    position,
):
    row_count = inputs.shape[0]
    heads_here = step_bias.shape[0]
    state_size = shared.shape[1] // 2
    values = jax.nn.silu(causal_filter(inputs, filter_weight, filter_bias, position)).reshape(
        row_count, heads_here, -1
    )
    factors = jax.nn.silu(causal_filter(shared, shared_filter, shared_filter_bias, position))
    writes = factors[:, :state_size]
    read_vectors = factors[:, state_size:]
    step_size = jax.nn.softplus(step_raw + step_bias)
    log_decay = -step_size * jnp.exp(decay_log)
    blocks = row_count // SPAN
    causal = jnp.arange(SPAN)[:, None] >= jnp.arange(SPAN)[None, :]

    def blocked(whole_array):
        return whole_array.reshape((blocks, SPAN) + whole_array.shape[1:])

    def span_step(state_carry, block_item):
        memory, last_segment = state_carry
        value_blk, write_blk, read_blk, size_blk, decay_blk, segment_blk = block_item
        cumulative = jnp.cumsum(decay_blk, axis=0).T
        inside = causal & (segment_blk[:, None] == segment_blk[None, :])
        spread = cumulative[:, :, None] - cumulative[:, None, :]
        decays = jnp.exp(jnp.where(inside[None], spread, -jnp.inf))
        scores = jnp.dot(read_blk, write_blk.T, precision=PRECISE)
        mixing = scores[None] * decays * size_blk.T[:, None, :]
        local_out = jnp.einsum("hts,shp->thp", mixing, value_blk, precision=PRECISE)
        carried = (segment_blk == last_segment).astype(value_blk.dtype)
        entering = jnp.exp(cumulative).T * carried[:, None]
        remote_out = (
            jnp.einsum("tn,hnp->thp", read_blk, memory, precision=PRECISE) * entering[:, :, None]
        )
        block_out = local_out + remote_out + skip_gain[None, :, None] * value_blk
        end_segment = segment_blk[-1]
        closing = (segment_blk == end_segment).astype(value_blk.dtype)
        weights = jnp.exp(cumulative[:, -1:] - cumulative) * size_blk.T * closing[None, :]
        added_state = jnp.einsum("sn,hs,shp->hnp", write_blk, weights, value_blk, precision=PRECISE)
        keeping = jnp.exp(cumulative[:, -1]) * (last_segment == end_segment).astype(value_blk.dtype)
        memory = memory * keeping[:, None, None] + added_state
        return ((memory, end_segment), block_out)

    initial = (jnp.zeros((heads_here, state_size, values.shape[2]), values.dtype), jnp.int32(-1))
    unused, outputs = lax.scan(
        jax.checkpoint(span_step),
        initial,
        (
            blocked(values),
            blocked(writes),
            blocked(read_vectors),
            blocked(step_size),
            blocked(log_decay),
            blocked(segment),
        ),
    )
    return outputs.reshape(row_count, -1)


def prenorm(hidden_in, norm_gain):
    scale = lax.rsqrt(jnp.mean(hidden_in * hidden_in, axis=1, keepdims=True) + EPSILON)
    return hidden_in * scale * norm_gain


def on_device(
    tokens,
    cotangent,
    destination,
    lengths,
    norm_gain,
    inner_weight,
    shared_weight,
    step_weight,
    filter_weight,
    filter_bias,
    shared_filter,
    shared_filter_bias,
    step_bias,
    decay_log,
    skip_gain,
    gate_gain,
    out_weight,
):
    row_count = tokens.shape[0]
    model_width = tokens.shape[1]
    group_rows = row_count // lax.axis_size("dp")
    my_index = lax.axis_index("dp")
    target_block = destination // row_count
    send_slot = (
        target_block * group_rows + (destination - target_block * row_count) - my_index * group_rows
    )
    send_order = (
        jnp.zeros((row_count,), jnp.int32).at[send_slot].set(jnp.arange(row_count, dtype=jnp.int32))
    )
    send_tokens = tokens[send_order]
    send_cot = cotangent[send_order]
    work_tokens, work_cot = (
        lax.all_to_all(send_tokens, "dp", split_axis=0, concat_axis=0, tiled=True),
        lax.all_to_all(send_cot, "dp", split_axis=0, concat_axis=0, tiled=True),
    )
    inner_full, shared_full, step_full, out_full = (
        lax.all_gather(inner_weight.astype(jnp.bfloat16), "dp", axis=0, tiled=True),
        lax.all_gather(shared_weight.astype(jnp.bfloat16), "dp", axis=0, tiled=True),
        lax.all_gather(step_weight.astype(jnp.bfloat16), "dp", axis=0, tiled=True),
        lax.all_gather(out_weight.astype(jnp.bfloat16), "dp", axis=0, tiled=True),
    )
    col_share = model_width // lax.axis_size("tensor")
    column = lax.axis_index("tensor") * col_share
    hidden_in = work_tokens.astype(jnp.float32)
    segment, position = segments_of(lengths[0], row_count)
    normed, pull_norm = jax.vjp(prenorm, hidden_in, norm_gain)
    normed_low = normed.astype(jnp.bfloat16)
    inner_flat = inner_full.reshape(inner_full.shape[0], -1)
    both = jnp.dot(normed_low, inner_flat, preferred_element_type=jnp.float32)
    half_width = both.shape[1] // 2
    gate_in = both[:, :half_width]
    inputs = both[:, half_width:]
    shared = jnp.dot(normed_low, shared_full, preferred_element_type=jnp.float32)
    step_raw = jnp.dot(normed_low, step_full, preferred_element_type=jnp.float32)

    def local_mixer(
        inputs,
        shared,
        step_raw,
        filter_weight,
        filter_bias,
        shared_filter,
        shared_filter_bias,
        step_bias,
        decay_log,
        skip_gain,
    ):
        return mixer(
            inputs,
            shared,
            step_raw,
            filter_weight,
            filter_bias,
            shared_filter,
            shared_filter_bias,
            step_bias,
            decay_log,
            skip_gain,
            segment,
            position,
        )

    mixed_in, pull_mixer = jax.vjp(
        local_mixer,
        inputs,
        shared,
        step_raw,
        filter_weight,
        filter_bias,
        shared_filter,
        shared_filter_bias,
        step_bias,
        decay_log,
        skip_gain,
    )
    gate_sig = jax.nn.sigmoid(gate_in)
    gate_act = gate_in * gate_sig
    gated = mixed_in * gate_act
    square_sum = lax.psum(jnp.sum(gated * gated, axis=1), "tensor")
    gate_scale = lax.rsqrt(square_sum / INNER + EPSILON)[:, None]
    gate_normed = (gated * gate_scale * gate_gain).astype(jnp.bfloat16)
    partial_out = jnp.einsum("ti,di->td", gate_normed, out_full, preferred_element_type=jnp.float32)
    branch = lax.psum(partial_out, "tensor")
    layer_work = (hidden_in + branch).astype(jnp.bfloat16)
    part_out = lax.dynamic_slice_in_dim(layer_work, column, col_share, 1)
    out_grad = jnp.einsum("td,ti->di", work_cot, gate_normed, preferred_element_type=jnp.float32)
    normed_grad = jnp.einsum("td,di->ti", work_cot, out_full, preferred_element_type=jnp.float32)
    gate_gain_grad = jnp.sum(normed_grad * gated * gate_scale, axis=0)
    scaled_grad = normed_grad * gate_gain
    cross_sum = lax.psum(jnp.sum(scaled_grad * gated, axis=1), "tensor")
    gated_grad = gate_scale * scaled_grad - gated * gate_scale**3 * (cross_sum / INNER)[:, None]
    mixed_grad = gated_grad * gate_act
    gate_in_grad = gated_grad * mixed_in * gate_sig * (1.0 + gate_in * (1.0 - gate_sig))
    (
        inputs_grad,
        shared_part,
        step_raw_grad,
        filter_weight_grad,
        filter_bias_grad,
        shared_filter_part,
        shared_bias_part,
        step_bias_grad,
        decay_log_grad,
        skip_gain_grad,
    ) = pull_mixer(mixed_grad)
    shared_grad, shared_filter_grad, shared_filter_bias_grad = lax.psum(
        (shared_part, shared_filter_part, shared_bias_part), "tensor"
    )
    both_low = jnp.concatenate([gate_in_grad, inputs_grad], axis=1).astype(jnp.bfloat16)
    shared_low = shared_grad.astype(jnp.bfloat16)
    step_low = step_raw_grad.astype(jnp.bfloat16)
    input_part = jnp.einsum("tk,dk->td", both_low, inner_flat, preferred_element_type=jnp.float32)
    input_part = input_part + jnp.einsum(
        "tk,dk->td", step_low, step_full, preferred_element_type=jnp.float32
    )
    normed_back = lax.psum(input_part, "tensor")
    normed_back = normed_back + jnp.einsum(
        "tk,dk->td", shared_low, shared_full, preferred_element_type=jnp.float32
    )
    input_norm_grad, norm_gain_grad = pull_norm(normed_back)
    input_work = (input_norm_grad + work_cot.astype(jnp.float32)).astype(jnp.bfloat16)
    part_grad = lax.dynamic_slice_in_dim(input_work, column, col_share, 1)
    inner_grad = jnp.einsum(
        "td,tk->dk", normed_low, both_low, preferred_element_type=jnp.float32
    ).reshape(inner_full.shape)
    shared_weight_grad = jnp.einsum(
        "td,tk->dk", normed_low, shared_low, preferred_element_type=jnp.float32
    )
    step_weight_grad = jnp.einsum(
        "td,tk->dk", normed_low, step_low, preferred_element_type=jnp.float32
    )
    inner_grad, shared_weight_grad, step_weight_grad, out_grad = (
        lax.psum_scatter(inner_grad, "dp", scatter_dimension=0, tiled=True),
        lax.psum_scatter(shared_weight_grad, "dp", scatter_dimension=0, tiled=True),
        lax.psum_scatter(step_weight_grad, "dp", scatter_dimension=0, tiled=True),
        lax.psum_scatter(out_grad, "dp", scatter_dimension=0, tiled=True),
    )
    (
        norm_gain_grad,
        filter_weight_grad,
        filter_bias_grad,
        shared_filter_grad,
        shared_filter_bias_grad,
        step_bias_grad,
        decay_log_grad,
        skip_gain_grad,
        gate_gain_grad,
    ) = lax.psum(
        (
            norm_gain_grad,
            filter_weight_grad,
            filter_bias_grad,
            shared_filter_grad,
            shared_filter_bias_grad,
            step_bias_grad,
            decay_log_grad,
            skip_gain_grad,
            gate_gain_grad,
        ),
        "dp",
    )
    part_out, part_grad = (
        lax.all_to_all(part_out, "dp", split_axis=0, concat_axis=0, tiled=True),
        lax.all_to_all(part_grad, "dp", split_axis=0, concat_axis=0, tiled=True),
    )
    back_out, back_grad = (
        lax.all_gather(part_out, "tensor", axis=1, tiled=True),
        lax.all_gather(part_grad, "tensor", axis=1, tiled=True),
    )
    layer_out = back_out[send_slot]
    input_grad = back_grad[send_slot]
    return (
        layer_out,
        input_grad,
        norm_gain_grad,
        inner_grad,
        shared_weight_grad,
        step_weight_grad,
        filter_weight_grad,
        filter_bias_grad,
        shared_filter_grad,
        shared_filter_bias_grad,
        step_bias_grad,
        decay_log_grad,
        skip_gain_grad,
        gate_gain_grad,
        out_grad,
    )


def solution(mesh):
    in_specs = (
        P("dp", None),
        P("dp", None),
        P("dp"),
        P("dp", None),
        P(),
        P("dp", None, "tensor"),
        P("dp", None),
        P("dp", "tensor"),
        P(None, "tensor"),
        P("tensor"),
        P(),
        P(),
        P("tensor"),
        P("tensor"),
        P("tensor"),
        P("tensor"),
        P("dp", "tensor"),
    )
    out_specs = (
        P("dp", None),
        P("dp", None),
        P(),
        P("dp", None, "tensor"),
        P("dp", None),
        P("dp", "tensor"),
        P(None, "tensor"),
        P("tensor"),
        P(),
        P(),
        P("tensor"),
        P("tensor"),
        P("tensor"),
        P("tensor"),
        P("dp", "tensor"),
    )
    return jax.shard_map(
        on_device, mesh=mesh, in_specs=in_specs, out_specs=out_specs, check_vma=False
    )
```

profile of v0, /device:TPU:0, one launch (start us, length us, event | category | flops | bytes accessed | tf_op | source)
XLA Modules:
  0.0 2527.5 jit_solution(8638867920375196014)
XLA Ops:
  19.1 17.3 gather_fusion
  42.7 88.8 %all-gather = bf16[8,192,12]{1,2,0:T(8,128)(2,1)S(1)} all-gather(bf16[1,192,12]{1,2,0:T(8,128)(2,1)S(1)} %convert_bitcast_fusion), channel_id=1, replica_groups=mesh['dp'=8,'tensor'=4] {'dp'}, dimensions={0}, use_global_device_ids=true | all-gather | bytes 41472 | tf_op jit(solution)/shard_map/all_gather | solution.py:146
  131.8 16.9 gather_fusion.2
  240.2 294.4 %while.47 = (s32[]{:T(128)}, f32[12,128,64]{1,2,0:T(8,128)S(1)}, s32[]{:T(128)}, f32[8,256,12,64]{1,0,3,2:T(8,128)}, f32[8,12,128,64]{2,3,1,0:T(8,128)}, /*index...) while((s32[]{:T(128)}, f32[12,128,64]{1,2,0:T(8,128)S(1)}, ...), condition=%wide.region_8.9_spmd.clone, body=%wide.region_5.8_spmd.clone.sunk | while | flops 1313649664 | bytes 11765497 | solution.py:87
  254.0 18.5 dynamic_update_slice.85
  290.8 18.5 dynamic_update_slice.85
  327.6 18.5 dynamic_update_slice.85
  364.4 18.5 dynamic_update_slice.85
  401.2 18.5 dynamic_update_slice.85
  438.0 18.5 dynamic_update_slice.85
  474.8 18.5 dynamic_update_slice.85
  511.6 18.5 dynamic_update_slice.85
  624.5 466.0 %while.48 = (s32[]{:T(128)}, f32[12]{0:T(128)}, f32[12,128,64]{1,2,0:T(8,128)S(1)}, f32[8,256,12,64]{1,0,3,2:T(8,128)}, f32[8,256,128]{2,1,0:T(8,128)}, /*index=...) while((s32[]{:T(128)}, f32[12]{0:T(128)}, ...), condition=%wide.region_27.28_spmd.clone, body=%wide.region_14.27_spmd.clone.sunk | while | flops 3037355008 | bytes 28656244 | solution.py:87
  657.0 18.5 dynamic_update_slice.89
  715.2 18.5 dynamic_update_slice.89
  773.4 18.5 dynamic_update_slice.89
  831.5 18.5 dynamic_update_slice.89
  889.7 18.5 dynamic_update_slice.89
  947.8 18.5 dynamic_update_slice.89
  1006.0 18.5 dynamic_update_slice.89
  1064.2 18.5 dynamic_update_slice.89
  1219.2 147.4 %all-reduce.31 = (bf16[2048,256]{1,0:T(8,128)(2,1)}, f32[4,256]{1,0:T(4,128)S(1)}, f32[256]{0:T(256)S(1)}) all-reduce(f32[2048,256]{1,0:T(8,128)S(1)} %fusion.111, f32[4,256]{1,0:T(4,128)S(1)} %pad_add_fusion.1, f32[256]{0:T(256)S(1)} %get-tuple-element.895), channel_id=1, replica_groups=mesh['dp'=8,'tensor'=4] {'tensor'}, use_global_device_ids=true, to_apply=%region_29.30 | all-reduce | flops 525568 | bytes 3155968 | tf_op jit(solution)/shard_map/psum | solution.py:233
  1366.6 702.3 %all-reduce.30.cloned.1.call-done = (f32[2048,1536]{1,0:T(8,128)}, f32[2048,1536]{1,0:T(8,128)}) async-done(((f32[2048,1536]{1,0:T(8,128)}, f32[2048,1536]{1,0:T(8,128)}), (f32[2048,1536]{1,0:T(8,128)}, f32[2048,1536]{1,0:T(8,128)})) %all-reduce.30.cloned.1.call-update) | async-done | bytes 25165840 | tf_op jit(solution)/shard_map/psum | solution.py:210
  2082.1 26.8 %all_to_all.45 = bf16[8,256,384]{2,1,0:T(8,128)(2,1)} all-to-all(bf16[8,256,384]{2,1,0:T(8,128)(2,1)S(1)} %bitcast.451), channel_id=1, replica_groups=mesh['dp'=8,'tensor'=4] {'dp'}, dimensions={0} | all-to-all | bytes 3145728 | tf_op jit(solution)/shard_map/all_to_all | solution.py:291
  2109.0 24.1 all_to_all.46
  2152.5 38.1 %reduce-scatter.7.cloned.1.call-done = f32[192,2,768]{2,0,1:T(8,128)} async-done(((f32[1536,2,768]{2,0,1:T(8,128)}), f32[192,2,768]{2,0,1:T(8,128)}) %reduce-scatter.7.cloned.1.call-update) | async-done | bytes 1179664 | tf_op jit(solution)/shard_map/reduce_scatter | solution.py:260
  2193.8 25.0 all-reduce.24
  2218.8 88.6 %all-gather.12.cloned.1.call-done = bf16[2048,1536]{1,0:T(8,128)(2,1)} async-done(((bf16[2048,384]{1,0:T(8,128)(2,1)}), bf16[2048,1536]{1,0:T(8,128)(2,1)}) %all-gather.12.cloned.1.call-update) | async-done | bytes 6291472 | tf_op jit(solution)/shard_map/all_gather | solution.py:295
  2307.4 16.8 gather_fusion.3
  2324.2 98.3 %all-gather.10.cloned.1.call-done = bf16[2048,1536]{1,0:T(8,128)(2,1)} async-done(((bf16[2048,384]{1,0:T(8,128)(2,1)}), bf16[2048,1536]{1,0:T(8,128)(2,1)}) %all-gather.10.cloned.1.call-update) | async-done | bytes 6291472 | tf_op jit(solution)/shard_map/all_gather | solution.py:294
  2439.3 23.6 reduce-scatter.9.cloned.1.call-done
  2462.9 57.8 %reduce-scatter.11.cloned.1.call-done = f32[192,768]{1,0:T(8,128)} async-done(((f32[1536,768]{1,0:T(8,128)}), f32[192,768]{1,0:T(8,128)}) %reduce-scatter.11.cloned.1.call-update) | async-done | bytes 589840 | tf_op jit(solution)/shard_map/reduce_scatter | solution.py:263
  (1035 shorter events, 820.6 us)
Async XLA Ops:
  7.2 182.1 %all-gather.6.cloned.1.call-start = ((), (), s32[]{:S(2)}) async-start(), calls=%async_computation.8 | async-start | bytes 5308416 | tf_op jit(solution)/shard_map/all_gather | solution.py:144
  36.4 95.1 %copy-start.73 = (f32[12]{0:T(128)S(1)}, f32[12]{0:T(128)}, u32[]{:S(2)}) copy-start(f32[12]{0:T(128)} %param.34) | copy-start | bytes 148
  36.4 122.0 %all-to-all-start = ((bf16[8,256,1536]{2,1,0:T(8,128)(2,1)}), bf16[8,256,1536]{2,1,0:T(8,128)(2,1)}, u32[]{:S(2)}, u32[]{:S(2)}) async-start(bf16[8,256,1536]{2,1,0:T(8,128)(2,1)} %bitcast.442), calls=%async_computation | async-start | bytes 12582912 | tf_op jit(solution)/shard_map/all_to_all | solution.py:140
  41.6 527.2 %all-gather.8.cloned.1.call-start = ((), (), s32[]{:S(2)}) async-start(), calls=%async_computation.9 | async-start | bytes 2654208 | tf_op jit(solution)/shard_map/all_gather | solution.py:147
  131.6 46.8 %copy-start.15 = (bf16[1536,12]{0,1:T(8,128)(2,1)}, bf16[1536,12]{0,1:T(8,128)(2,1)S(1)}, u32[]{:S(2)}) copy-start(bf16[1536,12]{0,1:T(8,128)(2,1)S(1)} %reshape.579) | copy-start | bytes 110596
  131.6 46.8 %copy-start.60 = (f32[12]{0:T(128)}, f32[12]{0:T(128)S(1)}, u32[]{:S(2)}) copy-start(f32[12]{0:T(128)S(1)} %exp.96) | copy-start | bytes 148
  148.8 62.9 %copy-start.37 = (f32[768]{0:T(1024)}, f32[768]{0:T(1024)S(1)}, u32[]{:S(2)}) copy-start(f32[768]{0:T(1024)S(1)} %get-tuple-element.897) | copy-start | bytes 9220
  148.8 62.8 %copy-start.39 = (f32[768]{0:T(1024)}, f32[768]{0:T(1024)S(1)}, u32[]{:S(2)}) copy-start(f32[768]{0:T(1024)S(1)} %get-tuple-element.898) | copy-start | bytes 9220
  148.8 62.8 %copy-start.41 = (f32[768]{0:T(1024)}, f32[768]{0:T(1024)S(1)}, u32[]{:S(2)}) copy-start(f32[768]{0:T(1024)S(1)} %get-tuple-element.899) | copy-start | bytes 9220
  148.8 62.8 %copy-start.43 = (f32[768]{0:T(1024)}, f32[768]{0:T(1024)S(1)}, u32[]{:S(2)}) copy-start(f32[768]{0:T(1024)S(1)} %get-tuple-element.896) | copy-start | bytes 9220
  158.4 53.3 %copy-start.17 = (f32[2048]{0:T(1024)}, f32[2048]{0:T(1024)S(1)}, u32[]{:S(2)}) copy-start(f32[2048]{0:T(1024)S(1)} %get-tuple-element.1029) | copy-start | bytes 24580
  158.4 53.3 %copy-start.19 = (f32[2048]{0:T(1024)}, f32[2048]{0:T(1024)S(1)}, u32[]{:S(2)}) copy-start(f32[2048]{0:T(1024)S(1)} %get-tuple-element.1030) | copy-start | bytes 24580
  158.4 53.3 %copy-start.21 = (f32[2048]{0:T(1024)}, f32[2048]{0:T(1024)S(1)}, u32[]{:S(2)}) copy-start(f32[2048]{0:T(1024)S(1)} %get-tuple-element.1031) | copy-start | bytes 24580
  158.4 410.3 %all-to-all-start.2 = ((bf16[8,256,1536]{2,1,0:T(8,128)(2,1)}), bf16[8,256,1536]{2,1,0:T(8,128)(2,1)}, u32[]{:S(2)}, u32[]{:S(2)}) async-start(bf16[8,256,1536]{2,1,0:T(8,128)(2,1)} %bitcast.441), calls=%async_computation.2 | async-start | bytes 12582912 | tf_op jit(solution)/shard_map/all_to_all | solution.py:141
  163.2 1905.6 %all-reduce.30.cloned.1.call-start = ((), (), s32[]{:S(2)}) async-start(), calls=%async_computation.16 | async-start | bytes 50331648 | tf_op jit(solution)/shard_map/psum | solution.py:210
  708.9 32.2 %copy-start.36 = (s32[8,256]{1,0:T(8,128)S(1)}, s32[8,256]{1,0:T(8,128)}, u32[]{:S(2)}) copy-start(s32[8,256]{1,0:T(8,128)} %copy-done.35) | copy-start | bytes 24580 | tf_op jit(solution)/shard_map/transpose(jvp())/while
  999.7 32.2 %copy-start.36 = (s32[8,256]{1,0:T(8,128)S(1)}, s32[8,256]{1,0:T(8,128)}, u32[]{:S(2)}) copy-start(s32[8,256]{1,0:T(8,128)} %copy-done.35) | copy-start | bytes 24580 | tf_op jit(solution)/shard_map/transpose(jvp())/while
  1057.9 32.2 %copy-start.36 = (s32[8,256]{1,0:T(8,128)S(1)}, s32[8,256]{1,0:T(8,128)}, u32[]{:S(2)}) copy-start(s32[8,256]{1,0:T(8,128)} %copy-done.35) | copy-start | bytes 24580 | tf_op jit(solution)/shard_map/transpose(jvp())/while
  1126.3 33.3 %slice-start = ((s8[6291456]{0:T(1024)(128)(4,1)}), s8[4194304]{0:T(1024)(128)(4,1)S(1)}, s32[]{:S(2)}) async-start(s8[6291456]{0:T(1024)(128)(4,1)} %bitcast.432), calls=%async_computation.17 | async-start | bytes 8388608
  1167.9 983.0 %reduce-scatter.13.cloned.1.call-start = ((), (), s32[]{:S(2)}) async-start(), calls=%async_computation.15 | async-start | bytes 884736
  1189.7 1000.9 %reduce-scatter.7.cloned.1.call-start = ((), (), s32[]{:S(2)}) async-start(), calls=%async_computation.12 | async-start | bytes 10616832 | tf_op jit(solution)/shard_map/reduce_scatter | solution.py:260
  1205.4 1102.0 %all-gather.12.cloned.1.call-start = ((), (), s32[]{:S(2)}) async-start(), calls=%async_computation.11 | async-start | bytes 7864320 | tf_op jit(solution)/shard_map/all_gather | solution.py:295
  1218.5 850.4 %copy-start.11 = (bf16[1536,256]{1,0:T(8,128)(2,1)S(1)}, bf16[1536,256]{1,0:T(8,128)(2,1)}, u32[]{:S(2)}) copy-start(bf16[1536,256]{1,0:T(8,128)(2,1)} %copy-done.10) | copy-start | bytes 2359300
  1218.5 850.4 %copy-start.29 = (f32[2048]{0:T(1024)S(1)}, f32[2048]{0:T(1024)}, u32[]{:S(2)}) copy-start(f32[2048]{0:T(1024)} %copy-done.28) | copy-start | bytes 24580
  1218.5 850.4 %copy-start.31 = (f32[1536]{0:T(1024)S(1)}, f32[1536]{0:T(1024)}, u32[]{:S(2)}) copy-start(f32[1536]{0:T(1024)} %param.25) | copy-start | bytes 18436
  2082.0 51.1 %copy-start.12 = (bf16[2048,256]{1,0:T(8,128)(2,1)S(1)}, bf16[2048,256]{1,0:T(8,128)(2,1)}, u32[]{:S(2)}) copy-start(bf16[2048,256]{1,0:T(8,128)(2,1)} %get-tuple-element.971) | copy-start | bytes 3145732
  2108.9 313.6 %all-gather.10.cloned.1.call-start = ((), (), s32[]{:S(2)}) async-start(), calls=%async_computation.10 | async-start | bytes 7864320 | tf_op jit(solution)/shard_map/all_gather | solution.py:294
  2133.1 329.8 %reduce-scatter.9.cloned.1.call-start = ((), (), s32[]{:S(2)}) async-start(), calls=%async_computation.13 | async-start | bytes 1769472 | tf_op jit(solution)/shard_map/reduce_scatter | solution.py:261
  2139.0 381.7 %reduce-scatter.11.cloned.1.call-start = ((), (), s32[]{:S(2)}) async-start(), calls=%async_computation.14 | async-start | bytes 5308416 | tf_op jit(solution)/shard_map/reduce_scatter | solution.py:263
  2150.7 43.0 %copy-start.49 = (f32[12]{0:T(128)S(1)}, f32[12]{0:T(128)}, u32[]{:S(2)}) copy-start(f32[12]{0:T(128)} %get-tuple-element.530) | copy-start | bytes 148
  2150.7 43.0 %copy-start.65 = (f32[768]{0:T(1024)S(1)}, f32[768]{0:T(1024)}, u32[]{:S(2)}) copy-start(f32[768]{0:T(1024)} %get-tuple-element.882) | copy-start | bytes 9220
  2150.7 156.6 %copy-start.34 = (s32[2048]{0:T(1024)S(1)}, s32[2048]{0:T(1024)}, u32[]{:S(2)}) copy-start(s32[2048]{0:T(1024)} %get-tuple-element.987) | copy-start | bytes 24580
  (105 other events, 1154.9 us)
Sparse Core Ops, SparseCore 0:
  10.4 46.6 all-gather.5
  59.0 70.6 all-gather.7
  1168.0 900.7 all-reduce.29
  2072.4 38.3 reduce-scatter.12
  2114.2 76.3 reduce-scatter.6
  2192.0 115.3 all-gather.11
  2308.9 113.5 all-gather.9
  2426.3 36.5 reduce-scatter.8
  2466.9 53.7 reduce-scatter.10
where the time goes:
time: 2550 us; the launch traced here: 2530 us
  waiting for transfers between devices  1010 us (40%)
  local copies, waits for them, and re-layouts  624 us (24%)
  blocking collectives  342 us (13%)
  matrix products  315 us (12%)
  other arithmetic  188 us (7%)
    psum x1, waiting for transfers between devices, on_device(): branch = lax.psum(partial_out, 'tensor')  702 us
    dynamic_update_slice x72, local copies, waits for them, and re-layouts, mixer(): lax.scan(jax.checkpoint(span_step), initial, (blocked(values), blocked(wr...  344 us
    psum x1, blocking collectives, on_device(): lax.psum((shared_part, shared_filter_part, shared_bias_part), 'tensor')  147 us
    dot_general x24, matrix products, span_step(): local_out = jnp.einsum('hts,shp->thp', mixing, value_blk, precision=PRECISE)  101 us
    all_gather x1, waiting for transfers between devices, on_device(): lax.all_gather(part_out, 'tensor', axis=1, tiled=True)  98.3 us
    all_gather x1, blocking collectives, on_device(): lax.all_gather(step_weight.astype(jnp.bfloat16), 'dp', axis=0, tiled=True)  88.8 us
    all_gather x1, waiting for transfers between devices, on_device(): lax.all_gather(part_grad, 'tensor', axis=1, tiled=True)  88.6 us
    reduce_scatter x1, waiting for transfers between devices, on_device(): lax.psum_scatter(out_grad, 'dp', scatter_dimension=0, tiled=True)  57.8 us
  transfers between devices with their start and end apart: 11, of which 6 were waited for; matrix products, arithmetic and copies ran while one was open for 21% of the time, Pallas kernels for 0%

commit v1 on v0

--- a/solution.py
+++ b/solution.py
@@ -207,7 +207,7 @@
     gate_scale = lax.rsqrt(square_sum / INNER + EPSILON)[:, None]
     gate_normed = (gated * gate_scale * gate_gain).astype(jnp.bfloat16)
     partial_out = jnp.einsum("ti,di->td", gate_normed, out_full, preferred_element_type=jnp.float32)
-    branch = lax.psum(partial_out, "tensor")
+    branch = jnp.sum(lax.all_gather(partial_out, "tensor"), axis=0)
     layer_work = (hidden_in + branch).astype(jnp.bfloat16)
     part_out = lax.dynamic_slice_in_dim(layer_work, column, col_share, 1)
     out_grad = jnp.einsum("td,ti->di", work_cot, gate_normed, preferred_element_type=jnp.float32)

time: 2550 us -> 2960 us (1.16)
  waiting for transfers between devices: 1010 us -> 1390 us
    all_gather x0 -> x1, waiting for transfers between devices: none -> 822 us  [on_device(): branch = jnp.sum(lax.all_gather(partial_out, 'tensor'), axis=0)]
    psum x1, waiting for transfers between devices: 702 us -> 284 us  [on_device(): normed_back = lax.psum(input_part, 'tensor')]
    reduce_scatter x1, waiting for transfers between devices: 38.1 us -> 0.01 us  [on_device(): lax.psum_scatter(inner_grad, 'dp', scatter_dimension=0, tiled=True)]
  transfers between devices with their start and end apart: 11 -> 12, of which waited for: 6 -> 6; matrix products, arithmetic and copies ran while one was open for 21% -> 20% of each run, Pallas kernels for 0% -> 0%
where the time goes in v1:
time: 2960 us; the launch traced here: 2940 us
  waiting for transfers between devices  1390 us (47%)
  local copies, waits for them, and re-layouts  625 us (21%)
  blocking collectives  346 us (12%)
  matrix products  315 us (11%)
  other arithmetic  209 us (7%)
    all_gather x1, waiting for transfers between devices, on_device(): branch = jnp.sum(lax.all_gather(partial_out, 'tensor'), axis=0)  822 us
    dynamic_update_slice x72, local copies, waits for them, and re-layouts, mixer(): lax.scan(jax.checkpoint(span_step), initial, (blocked(values), blocked(wr...  344 us
    psum x1, waiting for transfers between devices, on_device(): normed_back = lax.psum(input_part, 'tensor')  284 us
    psum x1, blocking collectives, on_device(): lax.psum((shared_part, shared_filter_part, shared_bias_part), 'tensor')  146 us
    all_gather x1, waiting for transfers between devices, on_device(): lax.all_gather(part_grad, 'tensor', axis=1, tiled=True)  109 us
    dot_general x24, matrix products, span_step(): local_out = jnp.einsum('hts,shp->thp', mixing, value_blk, precision=PRECISE)  101 us
    all_gather x1, waiting for transfers between devices, on_device(): lax.all_gather(part_out, 'tensor', axis=1, tiled=True)  98.3 us
    all_gather x1, blocking collectives, on_device(): lax.all_gather(step_weight.astype(jnp.bfloat16), 'dp', axis=0, tiled=True)  88.8 us
  transfers between devices with their start and end apart: 12, of which 6 were waited for; matrix products, arithmetic and copies ran while one was open for 20% of the time, Pallas kernels for 0%

profile of v1, /device:TPU:0, one launch (start us, length us, event | category | flops | bytes accessed | tf_op | source)
XLA Modules:
  0.0 2940.3 jit_solution(2497326627241442379)
XLA Ops:
  19.1 17.3 gather_fusion
  42.7 88.8 %all-gather.1 = bf16[8,192,12]{1,2,0:T(8,128)(2,1)S(1)} all-gather(bf16[1,192,12]{1,2,0:T(8,128)(2,1)S(1)} %convert_bitcast_fusion), channel_id=1, replica_groups=mesh['dp'=8,'tensor'=4] {'dp'}, dimensions={0}, use_global_device_ids=true | all-gather | bytes 41472 | tf_op jit(solution)/shard_map/all_gather | solution.py:146
  240.3 294.3 %while.47 = (s32[]{:T(128)}, f32[12,128,64]{1,2,0:T(8,128)S(1)}, s32[]{:T(128)}, f32[8,256,12,64]{1,0,3,2:T(8,128)}, f32[8,12,128,64]{2,3,1,0:T(8,128)}, /*index...) while((s32[]{:T(128)}, f32[12,128,64]{1,2,0:T(8,128)S(1)}, ...), condition=%wide.region_8.9_spmd.clone, body=%wide.region_5.8_spmd.clone.sunk | while | flops 1313649664 | bytes 11765497 | solution.py:87
  254.1 18.5 dynamic_update_slice.85
  290.9 18.5 dynamic_update_slice.85
  327.7 18.5 dynamic_update_slice.85
  364.5 18.5 dynamic_update_slice.85
  401.3 18.5 dynamic_update_slice.85
  438.1 18.5 dynamic_update_slice.85
  474.9 18.5 dynamic_update_slice.85
  511.7 18.5 dynamic_update_slice.85
  624.7 464.6 %while.48 = (s32[]{:T(128)}, f32[12]{0:T(128)}, f32[12,128,64]{1,2,0:T(8,128)S(1)}, f32[8,256,12,64]{1,0,3,2:T(8,128)}, f32[8,256,128]{2,1,0:T(8,128)}, /*index=...) while((s32[]{:T(128)}, f32[12]{0:T(128)}, ...), condition=%wide.region_27.28_spmd.clone, body=%wide.region_14.27_spmd.clone.sunk | while | flops 3037355008 | bytes 28656244 | solution.py:87
  657.1 18.5 dynamic_update_slice.89
  715.1 18.5 dynamic_update_slice.89
  773.1 18.5 dynamic_update_slice.89
  831.1 18.5 dynamic_update_slice.89
  889.0 18.5 dynamic_update_slice.89
  947.0 18.5 dynamic_update_slice.89
  1005.0 18.5 dynamic_update_slice.89
  1063.0 18.5 dynamic_update_slice.89
  1104.4 17.4 multiply_reduce_fusion.13
  1211.0 146.5 %all-reduce.30 = (bf16[2048,256]{1,0:T(8,128)(2,1)}, f32[4,256]{1,0:T(4,128)S(1)}, f32[256]{0:T(256)S(1)}) all-reduce(f32[2048,256]{1,0:T(8,128)S(1)} %fusion.111, f32[4,256]{1,0:T(4,128)S(1)} %pad_add_fusion.1, f32[256]{0:T(256)S(1)} %get-tuple-element.895), channel_id=1, replica_groups=mesh['dp'=8,'tensor'=4] {'tensor'}, use_global_device_ids=true, to_apply=%region_29.30 | all-reduce | flops 525568 | bytes 3155968 | tf_op jit(solution)/shard_map/psum | solution.py:233
  1357.5 284.5 %all-reduce.29.cloned.1.call-done = f32[2048,1536]{1,0:T(8,128)} async-done(((f32[2048,1536]{1,0:T(8,128)}), f32[2048,1536]{1,0:T(8,128)}) %all-reduce.29.cloned.1.call-update) | async-done | bytes 12582928 | tf_op jit(solution)/shard_map/psum | solution.py:243
  1656.5 821.8 %all-gather.16.cloned.1.call-done = f32[8192,1536]{1,0:T(8,128)} async-done(((f32[2048,1536]{1,0:T(8,128)}), f32[8192,1536]{1,0:T(8,128)}) %all-gather.16.cloned.1.call-update) | async-done | bytes 50331664 | tf_op jit(solution)/shard_map/all_gather | solution.py:210
  2478.3 24.7 reduce_sum.359
  2507.8 24.6 all_to_all.45
  2532.5 31.6 %all_to_all.46 = bf16[8,256,384]{2,1,0:T(8,128)(2,1)} all-to-all(bf16[8,256,384]{2,1,0:T(8,128)(2,1)S(1)} %bitcast.450), channel_id=1, replica_groups=mesh['dp'=8,'tensor'=4] {'dp'}, dimensions={0} | all-to-all | bytes 3145728 | tf_op jit(solution)/shard_map/all_to_all | solution.py:290
  2583.0 25.0 all-reduce.24
  2611.2 108.8 %all-gather.14.cloned.1.call-done = bf16[2048,1536]{1,0:T(8,128)(2,1)} async-done(((bf16[2048,384]{1,0:T(8,128)(2,1)}), bf16[2048,1536]{1,0:T(8,128)(2,1)}) %all-gather.14.cloned.1.call-update) | async-done | bytes 6291472 | tf_op jit(solution)/shard_map/all_gather | solution.py:295
  2736.8 98.3 %all-gather.12.cloned.1.call-done = bf16[2048,1536]{1,0:T(8,128)(2,1)} async-done(((bf16[2048,384]{1,0:T(8,128)(2,1)}), bf16[2048,1536]{1,0:T(8,128)(2,1)}) %all-gather.12.cloned.1.call-update) | async-done | bytes 6291472 | tf_op jit(solution)/shard_map/all_gather | solution.py:294
  2851.9 23.6 reduce-scatter.9.cloned.1.call-done
  2875.5 57.7 %reduce-scatter.11.cloned.1.call-done = f32[192,768]{1,0:T(8,128)} async-done(((f32[1536,768]{1,0:T(8,128)}), f32[192,768]{1,0:T(8,128)}) %reduce-scatter.11.cloned.1.call-update) | async-done | bytes 589840 | tf_op jit(solution)/shard_map/reduce_scatter | solution.py:263
  (1044 shorter events, 834.9 us)
Async XLA Ops:
  7.2 182.3 %all-gather.8.cloned.1.call-start = ((), (), s32[]{:S(2)}) async-start(), calls=%async_computation.8 | async-start | bytes 5308416 | tf_op jit(solution)/shard_map/all_gather | solution.py:144
  36.4 95.2 %copy-start.78 = (f32[12]{0:T(128)S(1)}, f32[12]{0:T(128)}, u32[]{:S(2)}) copy-start(f32[12]{0:T(128)} %param.34) | copy-start | bytes 148
  36.4 122.0 %all-to-all-start = ((bf16[8,256,1536]{2,1,0:T(8,128)(2,1)}), bf16[8,256,1536]{2,1,0:T(8,128)(2,1)}, u32[]{:S(2)}, u32[]{:S(2)}) async-start(bf16[8,256,1536]{2,1,0:T(8,128)(2,1)} %bitcast.442), calls=%async_computation | async-start | bytes 12582912 | tf_op jit(solution)/shard_map/all_to_all | solution.py:140
  41.6 527.3 %all-gather.10.cloned.1.call-start = ((), (), s32[]{:S(2)}) async-start(), calls=%async_computation.9 | async-start | bytes 2654208 | tf_op jit(solution)/shard_map/all_gather | solution.py:147
  131.6 47.0 %copy-start.15 = (bf16[1536,12]{0,1:T(8,128)(2,1)}, bf16[1536,12]{0,1:T(8,128)(2,1)S(1)}, u32[]{:S(2)}) copy-start(bf16[1536,12]{0,1:T(8,128)(2,1)S(1)} %reshape.580) | copy-start | bytes 110596
  131.6 47.0 %copy-start.65 = (f32[12]{0:T(128)}, f32[12]{0:T(128)S(1)}, u32[]{:S(2)}) copy-start(f32[12]{0:T(128)S(1)} %exp.96) | copy-start | bytes 148
  148.9 62.9 %copy-start.37 = (f32[768]{0:T(1024)}, f32[768]{0:T(1024)S(1)}, u32[]{:S(2)}) copy-start(f32[768]{0:T(1024)S(1)} %get-tuple-element.897) | copy-start | bytes 9220
  148.9 62.9 %copy-start.39 = (f32[768]{0:T(1024)}, f32[768]{0:T(1024)S(1)}, u32[]{:S(2)}) copy-start(f32[768]{0:T(1024)S(1)} %get-tuple-element.898) | copy-start | bytes 9220
  148.9 62.9 %copy-start.41 = (f32[768]{0:T(1024)}, f32[768]{0:T(1024)S(1)}, u32[]{:S(2)}) copy-start(f32[768]{0:T(1024)S(1)} %get-tuple-element.899) | copy-start | bytes 9220
  148.9 62.9 %copy-start.43 = (f32[768]{0:T(1024)}, f32[768]{0:T(1024)S(1)}, u32[]{:S(2)}) copy-start(f32[768]{0:T(1024)S(1)} %get-tuple-element.896) | copy-start | bytes 9220
  158.4 53.4 %copy-start.17 = (f32[2048]{0:T(1024)}, f32[2048]{0:T(1024)S(1)}, u32[]{:S(2)}) copy-start(f32[2048]{0:T(1024)S(1)} %get-tuple-element.1027) | copy-start | bytes 24580
  158.5 53.4 %copy-start.19 = (f32[2048]{0:T(1024)}, f32[2048]{0:T(1024)S(1)}, u32[]{:S(2)}) copy-start(f32[2048]{0:T(1024)S(1)} %get-tuple-element.1028) | copy-start | bytes 24580
  158.5 53.4 %copy-start.21 = (f32[2048]{0:T(1024)}, f32[2048]{0:T(1024)S(1)}, u32[]{:S(2)}) copy-start(f32[2048]{0:T(1024)S(1)} %get-tuple-element.1029) | copy-start | bytes 24580
  158.5 410.4 %all-to-all-start.2 = ((bf16[8,256,1536]{2,1,0:T(8,128)(2,1)}), bf16[8,256,1536]{2,1,0:T(8,128)(2,1)}, u32[]{:S(2)}, u32[]{:S(2)}) async-start(bf16[8,256,1536]{2,1,0:T(8,128)(2,1)} %bitcast.441), calls=%async_computation.2 | async-start | bytes 12582912 | tf_op jit(solution)/shard_map/all_to_all | solution.py:141
  163.3 1478.7 %all-reduce.29.cloned.1.call-start = ((), (), s32[]{:S(2)}) async-start(), calls=%async_computation.11 | async-start | bytes 25165824 | tf_op jit(solution)/shard_map/psum | solution.py:243
  650.8 32.1 %copy-start.36 = (s32[8,256]{1,0:T(8,128)S(1)}, s32[8,256]{1,0:T(8,128)}, u32[]{:S(2)}) copy-start(s32[8,256]{1,0:T(8,128)} %copy-done.35) | copy-start | bytes 24580 | tf_op jit(solution)/shard_map/transpose(jvp())/while
  708.8 32.1 %copy-start.36 = (s32[8,256]{1,0:T(8,128)S(1)}, s32[8,256]{1,0:T(8,128)}, u32[]{:S(2)}) copy-start(s32[8,256]{1,0:T(8,128)} %copy-done.35) | copy-start | bytes 24580 | tf_op jit(solution)/shard_map/transpose(jvp())/while
  824.7 32.1 %copy-start.36 = (s32[8,256]{1,0:T(8,128)S(1)}, s32[8,256]{1,0:T(8,128)}, u32[]{:S(2)}) copy-start(s32[8,256]{1,0:T(8,128)} %copy-done.35) | copy-start | bytes 24580 | tf_op jit(solution)/shard_map/transpose(jvp())/while
  940.7 32.1 %copy-start.36 = (s32[8,256]{1,0:T(8,128)S(1)}, s32[8,256]{1,0:T(8,128)}, u32[]{:S(2)}) copy-start(s32[8,256]{1,0:T(8,128)} %copy-done.35) | copy-start | bytes 24580 | tf_op jit(solution)/shard_map/transpose(jvp())/while
  998.7 32.1 %copy-start.36 = (s32[8,256]{1,0:T(8,128)S(1)}, s32[8,256]{1,0:T(8,128)}, u32[]{:S(2)}) copy-start(s32[8,256]{1,0:T(8,128)} %copy-done.35) | copy-start | bytes 24580 | tf_op jit(solution)/shard_map/transpose(jvp())/while
  1147.6 1330.7 %all-gather.16.cloned.1.call-start = ((), (), s32[]{:S(2)}) async-start(), calls=%async_computation.16 | async-start | bytes 62914560 | tf_op jit(solution)/shard_map/all_gather | solution.py:210
  1160.3 1421.1 %reduce-scatter.13.cloned.1.call-start = ((), (), s32[]{:S(2)}) async-start(), calls=%async_computation.17 | async-start | bytes 884736
  1181.5 1426.5 %reduce-scatter.7.cloned.1.call-start = ((), (), s32[]{:S(2)}) async-start(), calls=%async_computation.13 | async-start | bytes 10616832 | tf_op jit(solution)/shard_map/reduce_scatter | solution.py:260
  1197.3 1522.6 %all-gather.14.cloned.1.call-start = ((), (), s32[]{:S(2)}) async-start(), calls=%async_computation.12 | async-start | bytes 7864320 | tf_op jit(solution)/shard_map/all_gather | solution.py:295
  1210.3 431.7 %copy-start.11 = (bf16[1536,256]{1,0:T(8,128)(2,1)S(1)}, bf16[1536,256]{1,0:T(8,128)(2,1)}, u32[]{:S(2)}) copy-start(bf16[1536,256]{1,0:T(8,128)(2,1)} %copy-done.10) | copy-start | bytes 2359300
  1210.3 431.7 %copy-start.29 = (f32[2048]{0:T(1024)S(1)}, f32[2048]{0:T(1024)}, u32[]{:S(2)}) copy-start(f32[2048]{0:T(1024)} %copy-done.28) | copy-start | bytes 24580
  1210.3 431.7 %copy-start.31 = (f32[1536]{0:T(1024)S(1)}, f32[1536]{0:T(1024)}, u32[]{:S(2)}) copy-start(f32[1536]{0:T(1024)} %param.25) | copy-start | bytes 18436
  2507.8 56.3 %copy-start.12 = (bf16[2048,256]{1,0:T(8,128)(2,1)S(1)}, bf16[2048,256]{1,0:T(8,128)(2,1)}, u32[]{:S(2)}) copy-start(bf16[2048,256]{1,0:T(8,128)(2,1)} %get-tuple-element.971) | copy-start | bytes 3145732
  2532.5 302.6 %all-gather.12.cloned.1.call-start = ((), (), s32[]{:S(2)}) async-start(), calls=%async_computation.10 | async-start | bytes 7864320 | tf_op jit(solution)/shard_map/all_gather | solution.py:294
  2564.1 311.4 %reduce-scatter.9.cloned.1.call-start = ((), (), s32[]{:S(2)}) async-start(), calls=%async_computation.14 | async-start | bytes 1769472 | tf_op jit(solution)/shard_map/reduce_scatter | solution.py:261
  2570.2 363.0 %reduce-scatter.11.cloned.1.call-start = ((), (), s32[]{:S(2)}) async-start(), calls=%async_computation.15 | async-start | bytes 5308416 | tf_op jit(solution)/shard_map/reduce_scatter | solution.py:263
  2581.2 138.7 %copy-start.34 = (s32[2048]{0:T(1024)S(1)}, s32[2048]{0:T(1024)}, u32[]{:S(2)}) copy-start(s32[2048]{0:T(1024)} %get-tuple-element.985) | copy-start | bytes 24580
  (109 other events, 1108.1 us)
Sparse Core Ops, SparseCore 0:
  10.4 46.6 all-gather.7
  59.6 70.0 all-gather.9
  1147.8 494.1 all-reduce.28
  1643.4 834.8 all-gather.15
  2481.9 33.0 reduce-scatter.12
  2518.4 84.5 reduce-scatter.6
  2604.6 115.3 all-gather.13
  2721.5 113.5 all-gather.11
  2838.9 36.5 reduce-scatter.8
  2879.4 53.7 reduce-scatter.10
